TPU v7x, 256 devices: a whole 4x4x8 slice. The times are simulated.
256 devices in a mesh: zg: 16 (over z_lo, y, core), gx: 16 (over z_hi, x).
Axes of the slice: x: 4, y: 4, z: 8 (z_hi: 4, z_lo: 2; z = z_hi * 2 + z_lo), core: 2. Of those that a mesh axis runs over, the one named last changes fastest.
Arguments:
- observed: float32 [512, 1024, 256], P('zg', 'gx'), may hold values from 0.25 to 4
- kernel_x: float32 [33], replicated, may hold values from 0.2 to 1
- kernel_y: float32 [33], replicated, may hold values from 0.2 to 1
- kernel_z: float32 [65], replicated, may hold values from 0.2 to 1
Outputs:
- estimate: float32 [512, 1024, 256], P('zg', 'gx')
All inputs are finite; a program needn't handle non-finite values.
Results may differ from a plain program's by a relative error of at most 0.0001.
Values sent between devices are 32-bit elements; how exact they have to be, the bound alone decides.
A program may use at most 64 MiB of HBM per device.

v0:
```python
import jax
import jax.numpy as jnp
from jax import lax
from jax.sharding import PartitionSpec as P

ITERS = 2


def with_halo(x, sides, width):
    for axis, dim in sides:
        peers, length = (lax.axis_size(axis), x.shape[dim])
        up = [(i, (i + 1) % peers) for i in range(peers - 1)]
        down = [(j, i) for i, j in up]
        last = lax.slice_in_dim(x, length - width, length, axis=dim)
        leading = lax.slice_in_dim(x, 0, width, axis=dim)
        before = lax.ppermute(last, axis, up)
        after = lax.ppermute(leading, axis, down)
        x = jnp.concatenate([before, x, after], axis=dim)
    return x


def band(prof, n_out, n_in, offset):
    diff = (
        jnp.arange(n_in, dtype=jnp.int32)[None, :]
        - jnp.arange(n_out, dtype=jnp.int32)[:, None]
        + offset
    )

    def add_tap(tap, acc):
        return acc + jnp.where(diff == tap, prof[tap], 0.0)

    return lax.fori_loop(0, prof.shape[0], add_tap, jnp.zeros((n_out, n_in), jnp.float32))


def lateral(volume, mat_x, mat_y, half_x):
    hp = lax.Precision.HIGHEST
    padded = with_halo(volume, (("gx", 1),), half_x)
    out = jnp.einsum("ij,zjy->ziy", mat_x, padded, precision=hp)
    return jnp.einsum("zxj,ij->zxi", out, mat_y, precision=hp)


def axial(mat_z, volume):
    return jnp.einsum("ij,jxy->ixy", mat_z, volume, precision=lax.Precision.HIGHEST)


def shards(observed, kernel_x, kernel_y, kernel_z):
    prof_x = kernel_x / jnp.sum(kernel_x)
    prof_y = kernel_y / jnp.sum(kernel_y)
    prof_z = kernel_z / jnp.sum(kernel_z)
    slab_z, cols_x, size_y = observed.shape
    half_x = (prof_x.shape[0] - 1) // 2
    half_y = (prof_y.shape[0] - 1) // 2
    half_z = (prof_z.shape[0] - 1) // 2
    fwd_x = band(prof_x, cols_x, cols_x + 2 * half_x, 0)
    adj_x = band(prof_x[::-1], cols_x, cols_x + 2 * half_x, 0)
    fwd_y = band(prof_y, size_y, size_y, half_y)
    adj_y = band(prof_y[::-1], size_y, size_y, half_y)
    observed_col = lax.all_to_all(observed, "zg", split_axis=1, concat_axis=0, tiled=True)
    whole_z = observed_col.shape[0]
    fwd_z = band(prof_z, whole_z, whole_z, half_z)
    adj_z = band(prof_z[::-1], whole_z, whole_z, half_z)
    estimate = observed
    for step in range(ITERS):
        smeared = lateral(estimate, fwd_x, fwd_y, half_x)
        columns = lax.all_to_all(smeared, "zg", split_axis=1, concat_axis=0, tiled=True)
        blurred = axial(fwd_z, columns)
        ratio = observed_col / blurred
        back_col = axial(adj_z, ratio)
        back = lax.all_to_all(back_col, "zg", split_axis=0, concat_axis=1, tiled=True)
        correction = lateral(back, adj_x, adj_y, half_x)
        estimate = estimate * correction
    return estimate


def solution(mesh):
    return jax.shard_map(
        shards,
        mesh=mesh,
        in_specs=(P("zg", "gx", None), P(), P(), P()),
        out_specs=P("zg", "gx", None),
        check_vma=False,
    )
```

profile of v0, /device:TPU:102, one launch (start us, length us, event | category | flops | bytes accessed | tf_op | source)
XLA Modules:
  0.0 640.7 jit_solution(16492316351428571004)
XLA Ops:
  0.0 2.4 fusion.77
  2.4 5.4 collective-permute-start
  7.8 1.9 collective-permute-start.1
  9.7 2.5 copy.23
  12.3 6.1 all-to-all-start
  21.2 43.9 %while.87 = (s32[]{:T(128)}, f32[256,256]{1,0:T(8,128)S(1)}, f32[33]{0:T(128)S(1)}, s32[]{:T(128)}, s32[]{:T(128)}) while((s32[]{:T(128)}, f32[256,256]{1,0:T(8,128)S(1)}, f32[33]{0:T(128)S(1)}, s32[]{:T(128)}, s32[]{:T(128)}) %tuple.177), condition=%wide.region_10.11_spmd.clone, body=%wide.region_9.10_spmd.clone.sunk | while | flops 393219 | bytes 524387 | solution.py:32
  65.8 114.4 %while.85 = (s32[]{:T(128)}, f32[512,512]{1,0:T(8,128)S(1)}, f32[65]{0:T(128)S(1)}, s32[]{:T(128)}, s32[]{:T(128)}) while((s32[]{:T(128)}, f32[512,512]{1,0:T(8,128)S(1)}, f32[65]{0:T(128)S(1)}, s32[]{:T(128)}, s32[]{:T(128)}) %tuple.180), condition=%wide.region_4.5_spmd.clone, body=%wide.region_3.4_spmd.clone.sunk | while | flops 1572867 | bytes 2097251 | solution.py:32
  180.8 42.8 %while.86 = (s32[]{:T(128)}, f32[64,96]{1,0:T(8,128)S(1)}, f32[33]{0:T(128)S(1)}, s32[]{:T(128)}, s32[]{:T(128)}) while((s32[]{:T(128)}, f32[64,96]{1,0:T(8,128)S(1)}, f32[33]{0:T(128)S(1)}, s32[]{:T(128)}, s32[]{:T(128)}) %tuple.174), condition=%wide.region_7.8_spmd.clone, body=%wide.region_6.7_spmd.clone.sunk | while | flops 30723 | bytes 49251 | solution.py:32
  223.6 3.8 fusion.47
  227.4 4.2 fusion.42
  231.6 6.0 all-to-all-start.1
  237.7 113.3 %while.84 = (s32[]{:T(128)}, f32[512,512]{1,0:T(8,128)S(1)}, f32[65]{0:T(128)S(1)}, s32[]{:T(128)}, s32[]{:T(128)}) while((s32[]{:T(128)}, f32[512,512]{1,0:T(8,128)S(1)}, f32[65]{0:T(128)S(1)}, s32[]{:T(128)}, s32[]{:T(128)}) %tuple.183), condition=%wide.region_2.0_spmd.clone, body=%wide.region_1.0_spmd.clone.sunk | while | flops 1572867 | bytes 2097251 | solution.py:32
  238.3 1.1 select_add_fusion.12
  240.0 1.1 select_add_fusion.12
  241.7 1.1 select_add_fusion.12
  243.5 1.1 select_add_fusion.12
  245.2 1.1 select_add_fusion.12
  247.0 1.1 select_add_fusion.12
  248.7 1.1 select_add_fusion.12
  250.5 1.1 select_add_fusion.12
  252.2 1.1 select_add_fusion.12
  254.0 1.1 select_add_fusion.12
  255.7 1.1 select_add_fusion.12
  257.4 1.1 select_add_fusion.12
  269.6 1.1 select_add_fusion.12
  278.4 1.1 select_add_fusion.12
  302.8 1.1 select_add_fusion.12
  311.5 1.1 select_add_fusion.12
  335.9 1.1 select_add_fusion.12
  344.6 1.1 select_add_fusion.12
  351.0 3.2 copy.24
  354.2 2.0 copy.26
  356.4 3.7 bitcast_divide_fusion.1
  360.1 3.6 fusion.60
  363.7 2.6 copy.27
  366.3 5.7 all-to-all-start.2
  372.1 45.7 %while.89 = (s32[]{:T(128)}, f32[256,256]{1,0:T(8,128)S(1)}, f32[33]{0:T(128)S(1)}, s32[]{:T(128)}, s32[]{:T(128)}) while((s32[]{:T(128)}, f32[256,256]{1,0:T(8,128)S(1)}, f32[33]{0:T(128)S(1)}, s32[]{:T(128)}, s32[]{:T(128)}) %tuple.189), condition=%wide.region_14.15_spmd.clone, body=%wide.region_13.14_spmd.clone.sunk | while | flops 393219 | bytes 524387 | solution.py:32
  417.8 2.0 copy.28
  420.1 1.2 copy.30
  421.3 1.3 copy-done.2
  423.7 8.1 %collective-permute-start.2 = (f32[32,16,256]{2,1,0:T(8,128)}, f32[32,16,256]{2,1,0:T(8,128)S(1)}, u32[]{:S(2)}, u32[]{:S(2)}) collective-permute-start(f32[32,16,256]{2,1,0:T(8,128)} %get-tuple-element.609), channel_id=1, source_target_pairs={{0,1},{1,2},{2,3},{3,4},{4,5},{5,6},{6,7},{7,8},{8,9},{9,10},{10,1... | collective-permute-start | bytes 1572872 | tf_op jit(solution)/shard_map/ppermute | solution.py:16
  431.8 2.1 collective-permute-start.3
  434.0 44.7 %while.88 = (s32[]{:T(128)}, f32[64,96]{1,0:T(8,128)S(1)}, f32[33]{0:T(128)S(1)}, s32[]{:T(128)}, s32[]{:T(128)}) while((s32[]{:T(128)}, f32[64,96]{1,0:T(8,128)S(1)}, f32[33]{0:T(128)S(1)}, s32[]{:T(128)}, s32[]{:T(128)}) %tuple.186), condition=%wide.region_12.13_spmd.clone, body=%wide.region_11.12_spmd.clone.sunk | while | flops 30723 | bytes 49251 | solution.py:32
  478.7 3.9 fusion.18
  482.7 1.9 fusion.50
  484.7 8.1 %collective-permute-start.4 = (f32[32,16,256]{2,1,0:T(8,128)S(1)}, f32[32,16,256]{2,1,0:T(8,128)S(1)}, u32[]{:S(2)}, u32[]{:S(2)}) collective-permute-start(f32[32,16,256]{2,1,0:T(8,128)S(1)} %get-tuple-element.607), channel_id=1, source_target_pairs={{0,1},{1,2},{2,3},{3,4},{4,5},{5,6},{6,7},{7,8},{8,9},{9,10},{10,1... | collective-permute-start | bytes 1572872 | tf_op jit(solution)/shard_map/ppermute | solution.py:16
  492.8 1.9 collective-permute-start.5
  494.7 16.5 %collective-permute-done.4 = f32[32,16,256]{2,1,0:T(8,128)S(1)} collective-permute-done((f32[32,16,256]{2,1,0:T(8,128)S(1)}, f32[32,16,256]{2,1,0:T(8,128)S(1)}, u32[]{:S(2)}, u32[]{:S(2)}) %collective-permute-start.4) | collective-permute-done | bytes 524320 | tf_op jit(solution)/shard_map/ppermute | solution.py:16
  511.3 10.9 %collective-permute-done.5 = f32[32,16,256]{2,1,0:T(8,128)S(1)} collective-permute-done((f32[32,16,256]{2,1,0:T(8,128)S(1)}, f32[32,16,256]{2,1,0:T(8,128)S(1)}, u32[]{:S(2)}, u32[]{:S(2)}) %collective-permute-start.5) | collective-permute-done | bytes 524320 | tf_op jit(solution)/shard_map/ppermute | solution.py:17
  522.2 2.3 fusion.44
  524.5 3.0 fusion.40
  527.5 32.3 %all_to_all.90 = f32[32,64,256]{2,0,1:T(8,128)S(1)} all-to-all(f32[32,64,256]{2,0,1:T(8,128)S(1)} %fusion.40), channel_id=1, replica_groups=mesh['zg'=16,'gx'=16] {'zg'}, dimensions={1} | all-to-all | bytes 4194304 | tf_op jit(solution)/shard_map/all_to_all | solution.py:65
  560.0 1.4 copy-done.4
  561.4 3.7 bitcast_divide_fusion
  565.1 3.6 fusion.58
  568.7 1.4 copy.35
  570.0 30.3 %all_to_all.91 = f32[512,4,256]{2,1,0:T(4,128)S(1)} all-to-all(f32[512,4,256]{2,1,0:T(4,128)S(1)} %copy.35), channel_id=1, replica_groups=mesh['zg'=16,'gx'=16] {'zg'}, dimensions={0} | all-to-all | bytes 4194304 | tf_op jit(solution)/shard_map/all_to_all | solution.py:69
  600.9 1.2 copy.38
  602.2 1.9 collective-permute-start.6
  604.1 4.2 collective-permute-start.7
  608.3 14.1 %collective-permute-done.6 = f32[32,16,256]{2,1,0:T(8,128)S(1)} collective-permute-done((f32[32,16,256]{2,1,0:T(8,128)S(1)}, f32[32,16,256]{2,1,0:T(8,128)S(1)}, u32[]{:S(2)}, u32[]{:S(2)}) %collective-permute-start.6) | collective-permute-done | bytes 524320 | tf_op jit(solution)/shard_map/ppermute | solution.py:16
  622.4 12.2 %collective-permute-done.7 = f32[32,16,256]{2,1,0:T(8,128)S(1)} collective-permute-done((f32[32,16,256]{2,1,0:T(8,128)S(1)}, f32[32,16,256]{2,1,0:T(8,128)S(1)}, u32[]{:S(2)}, u32[]{:S(2)}) %collective-permute-start.7) | collective-permute-done | bytes 524320 | tf_op jit(solution)/shard_map/ppermute | solution.py:17
  634.7 2.3 fusion.30
  637.0 3.2 fusion.53
  (549 shorter events, 385.2 us)
Async XLA Ops:
  0.0 9.7 %copy-start = (f32[32,64,256]{2,1,0:T(8,128)S(1)}, f32[32,64,256]{2,1,0:T(8,128)}, u32[]{:S(2)}) copy-start(f32[32,64,256]{2,1,0:T(8,128)} %param.16) | copy-start | bytes 6291460
  2.4 221.1 %collective-permute-start = (f32[32,16,256]{2,1,0:T(8,128)}, f32[32,16,256]{2,1,0:T(8,128)S(1)}, u32[]{:S(2)}, u32[]{:S(2)}) collective-permute-start(f32[32,16,256]{2,1,0:T(8,128)} %get-tuple-element.611), channel_id=1, source_target_pairs={{0,1},{1,2},{2,3},{3,4},{4,5},{5,6},{6,7},{7,8},{8,9},{9,10},{10,1... | collective-permute-start | bytes 1572872 | tf_op jit(solution)/shard_map/ppermute | solution.py:16
  7.8 215.8 %collective-permute-start.1 = (f32[32,16,256]{2,1,0:T(8,128)}, f32[32,16,256]{2,1,0:T(8,128)}, u32[]{:S(2)}, u32[]{:S(2)}) collective-permute-start(f32[32,16,256]{2,1,0:T(8,128)} %get-tuple-element.612), channel_id=1, source_target_pairs={{1,0},{2,1},{3,2},{4,3},{5,4},{6,5},{7,6},{8,7},{9,8},{10,9},{11,1... | collective-permute-start | bytes 1572872 | tf_op jit(solution)/shard_map/ppermute | solution.py:17
  12.3 6.1 copy-start.7
  12.3 6.8 %copy-start.5 = (f32[33]{0:T(128)S(1)}, f32[33]{0:T(128)}, u32[]{:S(2)}) copy-start(f32[33]{0:T(128)} %param.18) | copy-start | bytes 400
  12.3 7.5 %copy-start.6 = (f32[65]{0:T(128)S(1)}, f32[65]{0:T(128)}, u32[]{:S(2)}) copy-start(f32[65]{0:T(128)} %param.19) | copy-start | bytes 784
  12.3 219.3 %all-to-all-start = ((f32[32,64,256]{2,0,1:T(8,128)}), f32[32,64,256]{2,0,1:T(8,128)}, u32[]{:S(2)}, u32[]{:S(2)}) async-start(f32[32,64,256]{2,0,1:T(8,128)} %copy.23), calls=%async_computation | async-start | bytes 4194304 | tf_op jit(solution)/shard_map/all_to_all | solution.py:58
  231.6 122.6 %all-to-all-start.1 = ((f32[32,64,256]{2,0,1:T(8,128)}), f32[32,64,256]{2,0,1:T(8,128)}, u32[]{:S(2)}, u32[]{:S(2)}) async-start(f32[32,64,256]{2,0,1:T(8,128)} %fusion.42), calls=%async_computation.1 | async-start | bytes 4194304 | tf_op jit(solution)/shard_map/all_to_all | solution.py:65
  354.2 2.2 copy-start.3
  366.3 51.5 %all-to-all-start.2 = ((f32[512,4,256]{2,1,0:T(4,128)}), f32[512,4,256]{2,1,0:T(4,128)}, u32[]{:S(2)}, u32[]{:S(2)}) async-start(f32[512,4,256]{2,1,0:T(4,128)} %copy.27), calls=%async_computation.2 | async-start | bytes 4194304 | tf_op jit(solution)/shard_map/all_to_all | solution.py:69
  421.3 1.3 copy-start.2
  423.7 55.0 %collective-permute-start.2 = (f32[32,16,256]{2,1,0:T(8,128)}, f32[32,16,256]{2,1,0:T(8,128)S(1)}, u32[]{:S(2)}, u32[]{:S(2)}) collective-permute-start(f32[32,16,256]{2,1,0:T(8,128)} %get-tuple-element.609), channel_id=1, source_target_pairs={{0,1},{1,2},{2,3},{3,4},{4,5},{5,6},{6,7},{7,8},{8,9},{9,10},{10,1... | collective-permute-start | bytes 1572872 | tf_op jit(solution)/shard_map/ppermute | solution.py:16
  431.8 46.9 %collective-permute-start.3 = (f32[32,16,256]{2,1,0:T(8,128)}, f32[32,16,256]{2,1,0:T(8,128)}, u32[]{:S(2)}, u32[]{:S(2)}) collective-permute-start(f32[32,16,256]{2,1,0:T(8,128)} %get-tuple-element.610), channel_id=1, source_target_pairs={{1,0},{2,1},{3,2},{4,3},{5,4},{6,5},{7,6},{8,7},{9,8},{10,9},{11,1... | collective-permute-start | bytes 1572872 | tf_op jit(solution)/shard_map/ppermute | solution.py:17
  478.7 3.9 copy-start.1
  484.7 26.6 %collective-permute-start.4 = (f32[32,16,256]{2,1,0:T(8,128)S(1)}, f32[32,16,256]{2,1,0:T(8,128)S(1)}, u32[]{:S(2)}, u32[]{:S(2)}) collective-permute-start(f32[32,16,256]{2,1,0:T(8,128)S(1)} %get-tuple-element.607), channel_id=1, source_target_pairs={{0,1},{1,2},{2,3},{3,4},{4,5},{5,6},{6,7},{7,8},{8,9},{9,10},{10,1... | collective-permute-start | bytes 1572872 | tf_op jit(solution)/shard_map/ppermute | solution.py:16
  492.8 29.4 %collective-permute-start.5 = (f32[32,16,256]{2,1,0:T(8,128)S(1)}, f32[32,16,256]{2,1,0:T(8,128)S(1)}, u32[]{:S(2)}, u32[]{:S(2)}) collective-permute-start(f32[32,16,256]{2,1,0:T(8,128)S(1)} %get-tuple-element.608), channel_id=1, source_target_pairs={{1,0},{2,1},{3,2},{4,3},{5,4},{6,5},{7,6},{8,7},{9,8},{10,9},{11,1... | collective-permute-start | bytes 1572872 | tf_op jit(solution)/shard_map/ppermute | solution.py:17
  559.8 1.6 copy-start.4
  602.2 20.2 %collective-permute-start.6 = (f32[32,16,256]{2,1,0:T(8,128)S(1)}, f32[32,16,256]{2,1,0:T(8,128)S(1)}, u32[]{:S(2)}, u32[]{:S(2)}) collective-permute-start(f32[32,16,256]{2,1,0:T(8,128)S(1)} %get-tuple-element.605), channel_id=1, source_target_pairs={{0,1},{1,2},{2,3},{3,4},{4,5},{5,6},{6,7},{7,8},{8,9},{9,10},{10,1... | collective-permute-start | bytes 1572872 | tf_op jit(solution)/shard_map/ppermute | solution.py:16
  604.1 30.5 %collective-permute-start.7 = (f32[32,16,256]{2,1,0:T(8,128)S(1)}, f32[32,16,256]{2,1,0:T(8,128)S(1)}, u32[]{:S(2)}, u32[]{:S(2)}) collective-permute-start(f32[32,16,256]{2,1,0:T(8,128)S(1)} %get-tuple-element.606), channel_id=1, source_target_pairs={{1,0},{2,1},{3,2},{4,3},{5,4},{6,5},{7,6},{8,7},{9,8},{10,9},{11,1... | collective-permute-start | bytes 1572872 | tf_op jit(solution)/shard_map/ppermute | solution.py:17
where the time goes:
time: 649 us; the launch traced here: 641 us
  other arithmetic  242 us (37%)
  local copies, waits for them, and re-layouts  185 us (29%)
  blocking collectives  62.6 us (10%)
  waiting for transfers between devices  53.8 us (8%)
  starting transfers between devices  51.6 us (8%)
  matrix products  39.1 us (6%)
    add x262, other arithmetic, add_tap(): return acc + jnp.where(diff == tap, prof[tap], 0.0)  238 us
    dynamic_slice x262, local copies, waits for them, and re-layouts, add_tap(): return acc + jnp.where(diff == tap, prof[tap], 0.0)  161 us
    all_to_all x1, blocking collectives, shards(): lax.all_to_all(smeared, 'zg', split_axis=1, concat_axis=0, tiled=True)  32.3 us
    ppermute x4, waiting for transfers between devices, with_halo(): before = lax.ppermute(last, axis, up)  30.6 us
    all_to_all x1, blocking collectives, shards(): lax.all_to_all(back_col, 'zg', split_axis=0, concat_axis=1, tiled=True)  30.3 us
    ppermute x4, starting transfers between devices, with_halo(): before = lax.ppermute(last, axis, up)  23.6 us
    ppermute x4, waiting for transfers between devices, with_halo(): after = lax.ppermute(leading, axis, down)  23.2 us
    dot_general x4, matrix products, axial(): jnp.einsum('ij,jxy->ixy', mat_z, volume, precision=lax.Precision.HIGHEST)  14.5 us
  transfers between devices with their start and end apart: 11, of which 4 were waited for; matrix products, arithmetic and copies ran while one was open for 65% of the time, Pallas kernels for 0%

commit v1 on v0

v1 whole, which is shorter than its diff:
```python
import functools

import jax
import jax.numpy as jnp
from jax import lax
from jax.experimental import pallas as pl
from jax.experimental.pallas import tpu as pltpu
from jax.sharding import PartitionSpec as P

STAGES = 4
CHUNKS = 4
MESH = pl.DeviceIdType.MESH
BF, F32 = jnp.bfloat16, jnp.float32


def split(v):
    hi = v.astype(BF)
    return hi, (v - hi.astype(F32)).astype(BF)


def mxu(a, b):
    return jnp.dot(a, b, preferred_element_type=F32)


def place(prof, width, step, start, rev):
    taps = prof.shape[1]
    h = prof / jnp.sum(prof)
    row = lax.broadcasted_iota(jnp.int32, (taps, width), 0)
    lane = lax.broadcasted_iota(jnp.int32, (taps, width), 1)
    t = (taps - 1 - row) if rev else row
    pick = jnp.where(lane == t * step + start, 1.0, 0.0).astype(F32)
    return lax.dot_general(
        jnp.broadcast_to(h, (8, taps)), pick, (((1,), (0,)), ((), ())),
        precision=lax.Precision.HIGHEST, preferred_element_type=F32,
    )[0:1]


def toeplitz(row, n):
    wide = jnp.broadcast_to(row, (n, row.shape[1]))
    return pltpu.roll(wide, 0, 1, stride=1, stride_axis=0)


def kernel(nz, nx, obs_ref, kx_ref, ky_ref, kz_ref, out_ref, comb, g, wz, wx, wyh, wyl,
           zsend, zrecv, xsend, xrecv):
    cols, slab, size_y = out_ref.shape
    part = cols // CHUNKS
    hz, hx = slab, part
    zg, gx = lax.axis_index("zg"), lax.axis_index("gx")
    odd = lax.rem(gx, 2)
    has_l, has_r = zg > 0, zg < nz - 1

    near = gx - 1 + 2 * odd
    far = gx + 1 - 2 * odd
    has_near = jnp.logical_and(gx > 0, gx < nx - 1)

    barrier = pltpu.get_barrier_semaphore()
    peers = (
        ((zg - 1, gx), has_l), ((zg + 1, gx), has_r), ((zg, near), has_near), ((zg, far), gx >= 0),
    )
    for peer, there in peers:
        @pl.when(there)
        def _():
            pl.semaphore_signal(barrier, inc=1, device_id=peer, device_id_type=MESH)

    def first(c):
        return part * (c + odd * (CHUNKS - 1 - 2 * c))

    def z_copy(s, c, side):
        rows = pl.ds(first(c), part)
        return pltpu.make_async_remote_copy(
            src_ref=comb.at[s, rows, pl.ds(hz, slab)],
            dst_ref=comb.at[s, rows, pl.ds((hz + slab) * (1 - side), slab)],
            send_sem=zsend.at[s, c, side], recv_sem=zrecv.at[s, c, side],
            device_id=(zg - 1 + 2 * side, gx), device_id_type=MESH,
        )

    def z_start(s, c):
        @pl.when(has_l)
        def _():
            z_copy(s, c, 0).start()

        @pl.when(has_r)
        def _():
            z_copy(s, c, 1).start()

    def x_copy(s, end):
        c = end * (CHUNKS - 1)
        low = (odd + end) % 2
        return pltpu.make_async_remote_copy(
            src_ref=g.at[s, pl.ds(hx + first(c), hx)],
            dst_ref=g.at[s, pl.ds((hx + cols) * (1 - low), hx)],
            send_sem=xsend.at[s, end], recv_sem=xrecv.at[s, end],
            device_id=(zg, near if end == 0 else far), device_id_type=MESH,
        )

    def z_pass(s, c):
        @pl.when(has_r)
        def _():
            z_copy(s, c, 0).wait_recv()

        @pl.when(has_l)
        def _():
            z_copy(s, c, 1).wait_recv()

        d = lax.rem(s, 2)
        both = wz[d]
        high = both[:slab]

        def column(i, _):
            hi, lo = split(comb[s, first(c) + i])
            top = mxu(both, hi)
            g[s, hx + first(c) + i] = top[:slab] + top[slab:] + mxu(high, lo)
            return 0

        lax.fori_loop(0, part, column, 0, unroll=4)
        if c == 0:
            @pl.when(has_near)
            def _():
                x_copy(s, 0).start()
        if c == CHUNKS - 1:
            x_copy(s, 1).start()

    def xy_pass(s, c):
        if c == 0:
            @pl.when(has_near)
            def _():
                x_copy(s, 0).wait_recv()
        if c == CHUNKS - 1:
            x_copy(s, 1).wait_recv()
        d = lax.rem(s, 2)
        rows = pl.ds(first(c), part)
        n = part * 8

        def group(k, _):
            zs = pl.ds(pl.multiple_of(k * 8, 8), 8)
            own = pl.ds(pl.multiple_of(hz + k * 8, 8), 8)
            hi, lo = split(g[s, pl.ds(first(c), part + 2 * hx), zs].reshape((part + 2 * hx) * 8, size_y))
            top = mxu(wx[d], hi)
            v = top[:n] + top[n:] + mxu(wx[d, :n], lo)
            hi, lo = split(v)
            v = mxu(hi, wyh[d]) + mxu(hi, wyl[d]) + mxu(lo, wyh[d])
            v = v.reshape(part, 8, size_y)

            @pl.when(d == 0)
            def _():
                comb[s + 1, rows, own] = comb[0, rows, own] / v

            @pl.when(s == 1)
            def _():
                comb[2, rows, own] = comb[0, rows, own] * v

            @pl.when(s == STAGES - 1)
            def _():
                out_ref[rows, zs] = comb[2, rows, own] * v

            return 0

        lax.fori_loop(0, slab // 8, group, 0)

        @pl.when(s < STAGES - 1)
        def _():
            z_start(s + 1, c)

    for c in range(CHUNKS):
        for x8 in range(0, part, 8):
            xs = pl.ds(pl.multiple_of(first(c) + x8, 8), 8)
            comb[0, xs, hz:hz + slab] = jnp.swapaxes(obs_ref[:, xs], 0, 1)
        if c == 0:
            pl.semaphore_wait(barrier, sum(there.astype(jnp.int32) for _, there in peers))
        z_start(0, c)

    for rev in (False, True):
        d = int(rev)
        hi, lo = split(toeplitz(place(kz_ref[...], 128, 1, 0, rev), slab)[:, :slab + 2 * hz])
        wz[d, :slab] = hi
        wz[d, slab:] = lo
        hi, lo = split(toeplitz(place(kx_ref[...], 8 * (part + 2 * hx), 8, 0, rev), part * 8))
        wx[d, :part * 8] = hi
        wx[d, part * 8:] = lo
        half = ky_ref.shape[1] // 2
        hi, lo = split(toeplitz(place(ky_ref[...], size_y + 256, 1, 128 - half, not rev), size_y)[:, 128:128 + size_y])
        wyh[d] = hi
        wyl[d] = lo

    def stage(s, _):
        zeros_z = jnp.zeros((1, hz, size_y), F32)
        zeros_x = jnp.zeros((1, slab, size_y), F32)

        def fill(there, ref, lo, n, zs, zeros):
            @pl.when(there)
            def _():
                def body(i, _):
                    ref[s, pl.ds(lo + i, 1), zs] = zeros
                    return 0
                lax.fori_loop(0, n, body, 0, unroll=4)

        fill(zg == 0, comb, 0, cols, pl.ds(0, hz), zeros_z)
        fill(zg == nz - 1, comb, 0, cols, pl.ds(hz + slab, hz), zeros_z)
        fill(gx == 0, g, 0, hx, pl.ds(0, slab), zeros_x)
        fill(gx == nx - 1, g, hx + cols, hx, pl.ds(0, slab), zeros_x)

        z_pass(s, 0)
        z_pass(s, 1)

        @pl.when(s > 0)
        def _():
            xy_pass(s - 1, CHUNKS - 1)

        z_pass(s, 2)
        xy_pass(s, 0)
        xy_pass(s, 1)
        z_pass(s, 3)
        xy_pass(s, 2)
        return 0

    lax.fori_loop(0, STAGES, stage, 0)
    xy_pass(STAGES - 1, CHUNKS - 1)

    def drain(s, _):
        for c in range(CHUNKS):
            @pl.when(has_l)
            def _():
                z_copy(s, c, 0).wait_send()

            @pl.when(has_r)
            def _():
                z_copy(s, c, 1).wait_send()

        @pl.when(has_near)
        def _():
            x_copy(s, 0).wait_send()

        x_copy(s, 1).wait_send()
        return 0

    lax.fori_loop(0, STAGES, drain, 0)


def shards(nz, nx, observed, kernel_x, kernel_y, kernel_z):
    slab, cols, size_y = observed.shape
    part = cols // CHUNKS
    wide = slab * 3
    out = pl.pallas_call(
        functools.partial(kernel, nz, nx),
        out_shape=jax.ShapeDtypeStruct((cols, slab, size_y), F32),
        in_specs=[pl.BlockSpec(memory_space=pltpu.VMEM)] * 4,
        out_specs=pl.BlockSpec(memory_space=pltpu.VMEM),
        scratch_shapes=[
            pltpu.VMEM((STAGES, cols, wide, size_y), F32),
            pltpu.VMEM((STAGES, cols + 2 * part, slab, size_y), F32),
            pltpu.VMEM((2, 2 * slab, wide), BF),
            pltpu.VMEM((2, 16 * part, 24 * part), BF),
            pltpu.VMEM((2, size_y, size_y), BF),
            pltpu.VMEM((2, size_y, size_y), BF),
            pltpu.SemaphoreType.DMA((STAGES, CHUNKS, 2)),
            pltpu.SemaphoreType.DMA((STAGES, CHUNKS, 2)),
            pltpu.SemaphoreType.DMA((STAGES, 2)),
            pltpu.SemaphoreType.DMA((STAGES, 2)),
        ],
        compiler_params=pltpu.CompilerParams(
            collective_id=0, has_side_effects=True, vmem_limit_bytes=56 * 2**20
        ),
        name="deconvolve",
    )(
        observed,
        kernel_x.reshape(1, -1), kernel_y.reshape(1, -1), kernel_z.reshape(1, -1),
    )
    return jnp.swapaxes(out, 0, 1)


def solution(mesh):
    return jax.shard_map(
        functools.partial(shards, mesh.shape["zg"], mesh.shape["gx"]),
        mesh=mesh,
        in_specs=(P("zg", "gx", None), P(), P(), P()),
        out_specs=P("zg", "gx", None),
        check_vma=False,
    )
```

time: 649 us -> 207 us (0.32)
  the two profiles are of different devices: /device:TPU:102 before, /device:TPU:100 now
where the time goes in v1:
time: 207 us; the launch traced here: 206 us
  Pallas kernels  202 us (98%)
  local copies, waits for them, and re-layouts  4.13 us (2%)
    pallas_call x1, Pallas kernels, shards(): pl.pallas_call(functools.partial(kernel, nz, nx), out_shape=jax.ShapeDtyp...  202 us

profile of v1, /device:TPU:100, one launch (start us, length us, event | category | flops | bytes accessed | tf_op | source)
XLA Modules:
  0.0 206.4 jit_solution(12996277362034144213)
XLA Ops:
  0.0 202.3 %deconvolve.1 = f32[64,32,256]{2,1,0:T(8,128)} custom-call(f32[32,64,256]{2,1,0:T(8,128)} %obs_ref.1, f32[1,33]{1,0:T(1,128)} %bitcast.5, f32[1,33]{1,0:T(1,128)} %bitcast.6, f32[1,65]{1,0:T(1,128)} %bitcast.7), custom_call_target="tpu_custom_call" | custom-call | tf_op jit(solution)/shard_map/deconvolve/pallas_call | solution.py:243
  202.3 4.1 %copy.5 = f32[32,64,256]{2,1,0:T(8,128)} copy(f32[32,64,256]{2,0,1:T(8,128)} %bitcast.4) | data formatting | bytes 4194304 | tf_op jit(solution)/shard_map/transpose | solution.py:268

commit v2 on v1

--- a/solution.py
+++ b/solution.py
@@ -9,6 +9,8 @@
 
 STAGES = 4
 CHUNKS = 4
+RING = 4
+Z_DIRECT, X_DIRECT = 8, 8
 MESH = pl.DeviceIdType.MESH
 BF, F32 = jnp.bfloat16, jnp.float32
 
@@ -40,8 +42,8 @@
     return pltpu.roll(wide, 0, 1, stride=1, stride_axis=0)
 
 
-def kernel(nz, nx, obs_ref, kx_ref, ky_ref, kz_ref, out_ref, comb, g, wz, wx, wyh, wyl,
-           zsend, zrecv, xsend, xrecv):
+def kernel(nz, nx, obs_ref, kx_ref, ky_ref, kz_ref, out_ref, comb, g, zfw, xfw, wz, wx, wyh, wyl,
+           zsend, zrecv, xsend, xrecv, zbsend, zbrecv, xbsend, xbrecv, xfsend, xfrecv):
     cols, slab, size_y = out_ref.shape
     part = cols // CHUNKS
     hz, hx = slab, part
@@ -53,9 +55,25 @@
     far = gx + 1 - 2 * odd
     has_near = jnp.logical_and(gx > 0, gx < nx - 1)
 
+    mid = nz // 2
+    seam_l, seam_r = zg == mid, zg == mid - 1
+    z_end = jnp.logical_or(zg == 0, zg == nz - 1)
+    z_seam = jnp.logical_or(seam_l, seam_r)
+    place_x = lax.rem(gx, RING)
+    low_x, high_x = place_x == 0, place_x == RING - 1
+    x_end = jnp.logical_or(low_x, high_x)
+    turn = (1 - 2 * odd) * (RING - 1)
+    over = RING * (1 - 2 * odd)
+    x_seam = jnp.logical_and(x_end, has_near)
+    x_forward = jnp.logical_and(x_end, jnp.logical_and(gx + over >= 0, gx + over < nx))
+    x_from = jnp.logical_and(x_end, jnp.logical_and(gx - over >= 0, gx - over < nx))
+
     barrier = pltpu.get_barrier_semaphore()
     peers = (
         ((zg - 1, gx), has_l), ((zg + 1, gx), has_r), ((zg, near), has_near), ((zg, far), gx >= 0),
+        ((jnp.where(z_end, mid, 0), gx), jnp.logical_or(z_end, z_seam)),
+        ((jnp.where(z_end, mid - 1, nz - 1), gx), jnp.logical_or(z_end, z_seam)),
+        ((zg, gx + turn), x_end), ((zg, gx + over), x_forward), ((zg, gx - over), x_from),
     )
     for peer, there in peers:
         @pl.when(there)
@@ -65,8 +83,8 @@
     def first(c):
         return part * (c + odd * (CHUNKS - 1 - 2 * c))
 
-    def z_copy(s, c, side):
-        rows = pl.ds(first(c), part)
+    def z_copy(s, c, side, n=part):
+        rows = pl.ds(first(c), n)
         return pltpu.make_async_remote_copy(
             src_ref=comb.at[s, rows, pl.ds(hz, slab)],
             dst_ref=comb.at[s, rows, pl.ds((hz + slab) * (1 - side), slab)],
@@ -74,34 +92,89 @@
             device_id=(zg - 1 + 2 * side, gx), device_id_type=MESH,
         )
 
+    def z_hop(s, c, side, hop):
+        rows = pl.ds(first(c) + Z_DIRECT, part - Z_DIRECT)
+        if hop == 0:
+            src, dst, to = comb.at[s, rows, pl.ds(hz, slab)], zfw.at[s, c], (nz - 1) * (1 - side)
+        else:
+            src, dst, to = zfw.at[s, c], comb.at[s, rows, pl.ds((hz + slab) * (1 - side), slab)], mid - 1 + side
+        return pltpu.make_async_remote_copy(
+            src_ref=src, dst_ref=dst, send_sem=zbsend.at[s, c], recv_sem=zbrecv.at[s, c],
+            device_id=(to, gx), device_id_type=MESH,
+        )
+
+    z_sides = ((0, has_l, seam_l, zg == nz - 1), (1, has_r, seam_r, zg == 0))
+
     def z_start(s, c):
-        @pl.when(has_l)
-        def _():
-            z_copy(s, c, 0).start()
-
-        @pl.when(has_r)
-        def _():
-            z_copy(s, c, 1).start()
-
-    def x_copy(s, end):
+        for side, there, seam, _ in z_sides:
+            @pl.when(jnp.logical_and(there, jnp.logical_not(seam)))
+            def _():
+                z_copy(s, c, side).start()
+
+            @pl.when(seam)
+            def _():
+                z_hop(s, c, side, 0).start()
+                z_copy(s, c, side, Z_DIRECT).start()
+
+    def z_sent(s, c):
+        for side, there, seam, forwards in z_sides:
+            @pl.when(jnp.logical_and(there, jnp.logical_not(seam)))
+            def _():
+                z_copy(s, c, side).wait_send()
+
+            @pl.when(seam)
+            def _():
+                z_hop(s, c, side, 0).wait_send()
+                z_copy(s, c, side, Z_DIRECT).wait_send()
+
+            @pl.when(forwards)
+            def _():
+                z_hop(s, c, side, 1).wait_send()
+
+    def z_arrived(s, c):
+        for side, _, _, forwards in z_sides:
+            @pl.when(forwards)
+            def _():
+                z_hop(s, c, side, 0).wait_recv()
+                z_hop(s, c, side, 1).start()
+
+        for side, there, seam in ((0, has_r, seam_r), (1, has_l, seam_l)):
+            @pl.when(jnp.logical_and(there, jnp.logical_not(seam)))
+            def _():
+                z_copy(s, c, side).wait_recv()
+
+            @pl.when(seam)
+            def _():
+                z_copy(s, c, side, Z_DIRECT).wait_recv()
+                z_hop(s, c, side, 1).wait_recv()
+
+    def x_hop(s, hop):
+        if hop == 0:
+            src, dst, to = g.at[s, pl.ds(hx + first(0) + X_DIRECT, hx - X_DIRECT)], xfw.at[s], gx + turn
+            sems = xbsend, xfrecv
+        else:
+            src, dst, to = xfw.at[s], g.at[s, pl.ds((hx + cols) * odd + X_DIRECT, hx - X_DIRECT)], gx + over
+            sems = xfsend, xbrecv
+        return pltpu.make_async_remote_copy(
+            src_ref=src, dst_ref=dst, send_sem=sems[0].at[s], recv_sem=sems[1].at[s],
+            device_id=(zg, to), device_id_type=MESH,
+        )
+
+    def x_copy(s, end, n=part):
         c = end * (CHUNKS - 1)
         low = (odd + end) % 2
         return pltpu.make_async_remote_copy(
-            src_ref=g.at[s, pl.ds(hx + first(c), hx)],
-            dst_ref=g.at[s, pl.ds((hx + cols) * (1 - low), hx)],
+            src_ref=g.at[s, pl.ds(hx + first(c), n)],
+            dst_ref=g.at[s, pl.ds((hx + cols) * (1 - low), n)],
             send_sem=xsend.at[s, end], recv_sem=xrecv.at[s, end],
             device_id=(zg, near if end == 0 else far), device_id_type=MESH,
         )
 
+    def near_plain():
+        return jnp.logical_and(has_near, jnp.logical_not(x_seam))
+
     def z_pass(s, c):
-        @pl.when(has_r)
-        def _():
-            z_copy(s, c, 0).wait_recv()
-
-        @pl.when(has_l)
-        def _():
-            z_copy(s, c, 1).wait_recv()
-
+        z_arrived(s, c)
         d = lax.rem(s, 2)
         both = wz[d]
         high = both[:slab]
@@ -114,17 +187,27 @@
 
         lax.fori_loop(0, part, column, 0, unroll=4)
         if c == 0:
-            @pl.when(has_near)
+            @pl.when(near_plain())
             def _():
                 x_copy(s, 0).start()
+
+            @pl.when(x_seam)
+            def _():
+                x_hop(s, 0).start()
+                x_copy(s, 0, X_DIRECT).start()
         if c == CHUNKS - 1:
             x_copy(s, 1).start()
 
     def xy_pass(s, c):
         if c == 0:
-            @pl.when(has_near)
+            @pl.when(near_plain())
             def _():
                 x_copy(s, 0).wait_recv()
+
+            @pl.when(x_seam)
+            def _():
+                x_copy(s, 0, X_DIRECT).wait_recv()
+                x_hop(s, 1).wait_recv()
         if c == CHUNKS - 1:
             x_copy(s, 1).wait_recv()
         d = lax.rem(s, 2)
@@ -202,6 +285,11 @@
         z_pass(s, 0)
         z_pass(s, 1)
 
+        @pl.when(x_forward)
+        def _():
+            x_hop(s, 0).wait_recv()
+            x_hop(s, 1).start()
+
         @pl.when(s > 0)
         def _():
             xy_pass(s - 1, CHUNKS - 1)
@@ -218,17 +306,20 @@
 
     def drain(s, _):
         for c in range(CHUNKS):
-            @pl.when(has_l)
-            def _():
-                z_copy(s, c, 0).wait_send()
-
-            @pl.when(has_r)
-            def _():
-                z_copy(s, c, 1).wait_send()
-
-        @pl.when(has_near)
+            z_sent(s, c)
+
+        @pl.when(near_plain())
         def _():
             x_copy(s, 0).wait_send()
+
+        @pl.when(x_seam)
+        def _():
+            x_copy(s, 0, X_DIRECT).wait_send()
+            x_hop(s, 0).wait_send()
+
+        @pl.when(x_forward)
+        def _():
+            x_hop(s, 1).wait_send()
 
         x_copy(s, 1).wait_send()
         return 0
@@ -248,6 +339,8 @@
         scratch_shapes=[
             pltpu.VMEM((STAGES, cols, wide, size_y), F32),
             pltpu.VMEM((STAGES, cols + 2 * part, slab, size_y), F32),
+            pltpu.VMEM((STAGES, CHUNKS, part - Z_DIRECT, slab, size_y), F32),
+            pltpu.VMEM((STAGES, part - X_DIRECT, slab, size_y), F32),
             pltpu.VMEM((2, 2 * slab, wide), BF),
             pltpu.VMEM((2, 16 * part, 24 * part), BF),
             pltpu.VMEM((2, size_y, size_y), BF),
@@ -256,6 +349,12 @@
             pltpu.SemaphoreType.DMA((STAGES, CHUNKS, 2)),
             pltpu.SemaphoreType.DMA((STAGES, 2)),
             pltpu.SemaphoreType.DMA((STAGES, 2)),
+            pltpu.SemaphoreType.DMA((STAGES, CHUNKS)),
+            pltpu.SemaphoreType.DMA((STAGES, CHUNKS)),
+            pltpu.SemaphoreType.DMA((STAGES,)),
+            pltpu.SemaphoreType.DMA((STAGES,)),
+            pltpu.SemaphoreType.DMA((STAGES,)),
+            pltpu.SemaphoreType.DMA((STAGES,)),
         ],
         compiler_params=pltpu.CompilerParams(
             collective_id=0, has_side_effects=True, vmem_limit_bytes=56 * 2**20

time: 207 us -> 163 us (0.79)
  the two profiles are of different devices: /device:TPU:100 before, /device:TPU:98 now
where the time goes in v2:
time: 163 us; the launch traced here: 161 us
  Pallas kernels  157 us (96%)
  local copies, waits for them, and re-layouts  4.13 us (3%)
    pallas_call x1, Pallas kernels, shards(): pl.pallas_call(functools.partial(kernel, nz, nx), out_shape=jax.ShapeDtyp...  157 us
    transpose x1, local copies, waits for them, and re-layouts, shards(): return jnp.swapaxes(out, 0, 1)  4.13 us

profile of v2, /device:TPU:98, one launch (start us, length us, event | category | flops | bytes accessed | tf_op | source)
XLA Modules:
  0.0 160.8 jit_solution(1866507660795794472)
XLA Ops:
  0.0 156.7 %deconvolve.1 = f32[64,32,256]{2,1,0:T(8,128)} custom-call(f32[32,64,256]{2,1,0:T(8,128)} %obs_ref.1, f32[1,33]{1,0:T(1,128)} %bitcast.5, f32[1,33]{1,0:T(1,128)} %bitcast.6, f32[1,65]{1,0:T(1,128)} %bitcast.7), custom_call_target="tpu_custom_call" | custom-call | tf_op jit(solution)/shard_map/deconvolve/pallas_call | solution.py:334
  156.7 4.1 %copy.5 = f32[32,64,256]{2,1,0:T(8,128)} copy(f32[32,64,256]{2,0,1:T(8,128)} %bitcast.4) | data formatting | bytes 4194304 | tf_op jit(solution)/shard_map/transpose | solution.py:367

commit v3 on v2

--- a/solution.py
+++ b/solution.py
@@ -9,8 +9,10 @@
 
 STAGES = 4
 CHUNKS = 4
+PIECES = 8
+PER = PIECES // CHUNKS
 RING = 4
-Z_DIRECT, X_DIRECT = 8, 8
+Z_DIRECT, X_DIRECT = 4, 5
 MESH = pl.DeviceIdType.MESH
 BF, F32 = jnp.bfloat16, jnp.float32
 
@@ -43,9 +45,9 @@
 
 
 def kernel(nz, nx, obs_ref, kx_ref, ky_ref, kz_ref, out_ref, comb, g, zfw, xfw, wz, wx, wyh, wyl,
-           zsend, zrecv, xsend, xrecv, zbsend, zbrecv, xbsend, xbrecv, xfsend, xfrecv):
-    cols, slab, size_y = out_ref.shape
-    part = cols // CHUNKS
+           zsend, zrecv, xsend, xrecv, zbsend, zbrecv, xbsend, xbrecv, xfsend, xfrecv, xdone):
+    slab, cols, size_y = out_ref.shape
+    part, piece = cols // CHUNKS, cols // PIECES
     hz, hx = slab, part
     zg, gx = lax.axis_index("zg"), lax.axis_index("gx")
     odd = lax.rem(gx, 2)
@@ -83,8 +85,11 @@
     def first(c):
         return part * (c + odd * (CHUNKS - 1 - 2 * c))
 
-    def z_copy(s, c, side, n=part):
-        rows = pl.ds(first(c), n)
+    def head(p):
+        return piece * (p + odd * (PIECES - 1 - 2 * p))
+
+    def z_copy(s, c, side, n=piece):
+        rows = pl.ds(head(c), n)
         return pltpu.make_async_remote_copy(
             src_ref=comb.at[s, rows, pl.ds(hz, slab)],
             dst_ref=comb.at[s, rows, pl.ds((hz + slab) * (1 - side), slab)],
@@ -93,7 +98,7 @@
         )
 
     def z_hop(s, c, side, hop):
-        rows = pl.ds(first(c) + Z_DIRECT, part - Z_DIRECT)
+        rows = pl.ds(head(c) + Z_DIRECT, piece - Z_DIRECT)
         if hop == 0:
             src, dst, to = comb.at[s, rows, pl.ds(hz, slab)], zfw.at[s, c], (nz - 1) * (1 - side)
         else:
@@ -148,30 +153,39 @@
                 z_copy(s, c, side, Z_DIRECT).wait_recv()
                 z_hop(s, c, side, 1).wait_recv()
 
-    def x_hop(s, hop):
+    def x_hop(s, p, hop):
+        n = piece - X_DIRECT
         if hop == 0:
-            src, dst, to = g.at[s, pl.ds(hx + first(0) + X_DIRECT, hx - X_DIRECT)], xfw.at[s], gx + turn
+            src, dst, to = g.at[s, pl.ds(hx + head(p) + X_DIRECT, n)], xfw.at[s, p], gx + turn
             sems = xbsend, xfrecv
         else:
-            src, dst, to = xfw.at[s], g.at[s, pl.ds((hx + cols) * odd + X_DIRECT, hx - X_DIRECT)], gx + over
+            at = (1 - odd) * (hx - piece * (p + 1)) + odd * (hx + cols + piece * p)
+            src, dst, to = xfw.at[s, p], g.at[s, pl.ds(at + X_DIRECT, n)], gx + over
             sems = xfsend, xbrecv
         return pltpu.make_async_remote_copy(
-            src_ref=src, dst_ref=dst, send_sem=sems[0].at[s], recv_sem=sems[1].at[s],
+            src_ref=src, dst_ref=dst, send_sem=sems[0].at[s, p], recv_sem=sems[1].at[s, p],
             device_id=(zg, to), device_id_type=MESH,
         )
 
-    def x_copy(s, end, n=part):
-        c = end * (CHUNKS - 1)
+    def x_copy(s, end, p, n=piece):
+        at = head(p + end * (PIECES - PER))
         low = (odd + end) % 2
+        to = at + (hx + cols) * (1 - low) - (cols - hx) * low
         return pltpu.make_async_remote_copy(
-            src_ref=g.at[s, pl.ds(hx + first(c), n)],
-            dst_ref=g.at[s, pl.ds((hx + cols) * (1 - low), n)],
-            send_sem=xsend.at[s, end], recv_sem=xrecv.at[s, end],
+            src_ref=g.at[s, pl.ds(hx + at, n)],
+            dst_ref=g.at[s, pl.ds(to, n)],
+            send_sem=xsend.at[s, end, p], recv_sem=xrecv.at[s, end, p],
             device_id=(zg, near if end == 0 else far), device_id_type=MESH,
         )
 
     def near_plain():
         return jnp.logical_and(has_near, jnp.logical_not(x_seam))
+
+    def x_forward_on(s, p):
+        @pl.when(x_forward)
+        def _():
+            x_hop(s, p, 0).wait_recv()
+            x_hop(s, p, 1).start()
 
     def z_pass(s, c):
         z_arrived(s, c)
@@ -180,74 +194,76 @@
         high = both[:slab]
 
         def column(i, _):
-            hi, lo = split(comb[s, first(c) + i])
+            hi, lo = split(comb[s, head(c) + i])
             top = mxu(both, hi)
-            g[s, hx + first(c) + i] = top[:slab] + top[slab:] + mxu(high, lo)
+            g[s, hx + head(c) + i] = top[:slab] + top[slab:] + mxu(high, lo)
             return 0
 
-        lax.fori_loop(0, part, column, 0, unroll=4)
-        if c == 0:
+        lax.fori_loop(0, piece, column, 0, unroll=8)
+        if c < PER:
             @pl.when(near_plain())
             def _():
-                x_copy(s, 0).start()
+                x_copy(s, 0, c).start()
 
             @pl.when(x_seam)
             def _():
-                x_hop(s, 0).start()
-                x_copy(s, 0, X_DIRECT).start()
-        if c == CHUNKS - 1:
-            x_copy(s, 1).start()
+                x_hop(s, c, 0).start()
+                x_copy(s, 0, c, X_DIRECT).start()
+        if c >= PIECES - PER:
+            x_copy(s, 1, c - (PIECES - PER)).start()
 
     def xy_pass(s, c):
         if c == 0:
-            @pl.when(near_plain())
-            def _():
-                x_copy(s, 0).wait_recv()
-
-            @pl.when(x_seam)
-            def _():
-                x_copy(s, 0, X_DIRECT).wait_recv()
-                x_hop(s, 1).wait_recv()
+            for p in range(PER):
+                @pl.when(near_plain())
+                def _():
+                    x_copy(s, 0, p).wait_recv()
+
+                @pl.when(x_seam)
+                def _():
+                    x_copy(s, 0, p, X_DIRECT).wait_recv()
+                    x_hop(s, p, 1).wait_recv()
         if c == CHUNKS - 1:
-            x_copy(s, 1).wait_recv()
+            for p in range(PER):
+                x_copy(s, 1, p).wait_recv()
         d = lax.rem(s, 2)
         rows = pl.ds(first(c), part)
         n = part * 8
 
         def group(k, _):
             zs = pl.ds(pl.multiple_of(k * 8, 8), 8)
-            own = pl.ds(pl.multiple_of(hz + k * 8, 8), 8)
             hi, lo = split(g[s, pl.ds(first(c), part + 2 * hx), zs].reshape((part + 2 * hx) * 8, size_y))
             top = mxu(wx[d], hi)
             v = top[:n] + top[n:] + mxu(wx[d, :n], lo)
-            hi, lo = split(v)
-            v = mxu(hi, wyh[d]) + mxu(hi, wyl[d]) + mxu(lo, wyh[d])
-            v = v.reshape(part, 8, size_y)
-
-            @pl.when(d == 0)
-            def _():
-                comb[s + 1, rows, own] = comb[0, rows, own] / v
-
-            @pl.when(s == 1)
-            def _():
-                comb[2, rows, own] = comb[0, rows, own] * v
-
-            @pl.when(s == STAGES - 1)
-            def _():
-                out_ref[rows, zs] = comb[2, rows, own] * v
-
+            xdone[:, zs] = v.reshape(part, 8, size_y)
             return 0
 
-        lax.fori_loop(0, slab // 8, group, 0)
+        lax.fori_loop(0, slab // 8, group, 0, unroll=4)
+        hi, lo = split(xdone[...].reshape(part * slab, size_y))
+        v = mxu(hi, wyh[d]) + mxu(lo, wyh[d]) + mxu(hi, wyl[d])
+        v = v.reshape(part, slab, size_y)
+        own = pl.ds(hz, slab)
+
+        @pl.when(d == 0)
+        def _():
+            comb[s + 1, rows, own] = comb[0, rows, own] / v
+
+        @pl.when(s == 1)
+        def _():
+            comb[2, rows, own] = comb[0, rows, own] * v
+
+        @pl.when(s == STAGES - 1)
+        def _():
+            out_ref[:, pl.ds(pl.multiple_of(first(c), part), part)] = jnp.swapaxes(comb[2, rows, own] * v, 0, 1)
 
         @pl.when(s < STAGES - 1)
         def _():
-            z_start(s + 1, c)
-
-    for c in range(CHUNKS):
-        for x8 in range(0, part, 8):
-            xs = pl.ds(pl.multiple_of(first(c) + x8, 8), 8)
-            comb[0, xs, hz:hz + slab] = jnp.swapaxes(obs_ref[:, xs], 0, 1)
+            for p in range(PER):
+                z_start(s + 1, c * PER + p)
+
+    for c in range(PIECES):
+        xs = pl.ds(pl.multiple_of(head(c), piece), piece)
+        comb[0, xs, hz:hz + slab] = jnp.swapaxes(obs_ref[:, xs], 0, 1)
         if c == 0:
             pl.semaphore_wait(barrier, sum(there.astype(jnp.int32) for _, there in peers))
         z_start(0, c)
@@ -284,20 +300,21 @@
 
         z_pass(s, 0)
         z_pass(s, 1)
-
-        @pl.when(x_forward)
-        def _():
-            x_hop(s, 0).wait_recv()
-            x_hop(s, 1).start()
+        x_forward_on(s, 0)
+        z_pass(s, 2)
+        x_forward_on(s, 1)
 
         @pl.when(s > 0)
         def _():
             xy_pass(s - 1, CHUNKS - 1)
 
-        z_pass(s, 2)
+        z_pass(s, 3)
+        z_pass(s, 4)
         xy_pass(s, 0)
+        z_pass(s, 5)
         xy_pass(s, 1)
-        z_pass(s, 3)
+        z_pass(s, 6)
+        z_pass(s, 7)
         xy_pass(s, 2)
         return 0
 
@@ -305,23 +322,24 @@
     xy_pass(STAGES - 1, CHUNKS - 1)
 
     def drain(s, _):
-        for c in range(CHUNKS):
+        for c in range(PIECES):
             z_sent(s, c)
 
-        @pl.when(near_plain())
-        def _():
-            x_copy(s, 0).wait_send()
-
-        @pl.when(x_seam)
-        def _():
-            x_copy(s, 0, X_DIRECT).wait_send()
-            x_hop(s, 0).wait_send()
-
-        @pl.when(x_forward)
-        def _():
-            x_hop(s, 1).wait_send()
-
-        x_copy(s, 1).wait_send()
+        for p in range(PER):
+            @pl.when(near_plain())
+            def _():
+                x_copy(s, 0, p).wait_send()
+
+            @pl.when(x_seam)
+            def _():
+                x_copy(s, 0, p, X_DIRECT).wait_send()
+                x_hop(s, p, 0).wait_send()
+
+            @pl.when(x_forward)
+            def _():
+                x_hop(s, p, 1).wait_send()
+
+            x_copy(s, 1, p).wait_send()
         return 0
 
     lax.fori_loop(0, STAGES, drain, 0)
@@ -329,32 +347,33 @@
 
 def shards(nz, nx, observed, kernel_x, kernel_y, kernel_z):
     slab, cols, size_y = observed.shape
-    part = cols // CHUNKS
+    part, piece = cols // CHUNKS, cols // PIECES
     wide = slab * 3
     out = pl.pallas_call(
         functools.partial(kernel, nz, nx),
-        out_shape=jax.ShapeDtypeStruct((cols, slab, size_y), F32),
+        out_shape=jax.ShapeDtypeStruct((slab, cols, size_y), F32),
         in_specs=[pl.BlockSpec(memory_space=pltpu.VMEM)] * 4,
         out_specs=pl.BlockSpec(memory_space=pltpu.VMEM),
         scratch_shapes=[
             pltpu.VMEM((STAGES, cols, wide, size_y), F32),
             pltpu.VMEM((STAGES, cols + 2 * part, slab, size_y), F32),
-            pltpu.VMEM((STAGES, CHUNKS, part - Z_DIRECT, slab, size_y), F32),
-            pltpu.VMEM((STAGES, part - X_DIRECT, slab, size_y), F32),
+            pltpu.VMEM((STAGES, PIECES, piece - Z_DIRECT, slab, size_y), F32),
+            pltpu.VMEM((STAGES, PER, piece - X_DIRECT, slab, size_y), F32),
             pltpu.VMEM((2, 2 * slab, wide), BF),
             pltpu.VMEM((2, 16 * part, 24 * part), BF),
             pltpu.VMEM((2, size_y, size_y), BF),
             pltpu.VMEM((2, size_y, size_y), BF),
-            pltpu.SemaphoreType.DMA((STAGES, CHUNKS, 2)),
-            pltpu.SemaphoreType.DMA((STAGES, CHUNKS, 2)),
-            pltpu.SemaphoreType.DMA((STAGES, 2)),
-            pltpu.SemaphoreType.DMA((STAGES, 2)),
-            pltpu.SemaphoreType.DMA((STAGES, CHUNKS)),
-            pltpu.SemaphoreType.DMA((STAGES, CHUNKS)),
-            pltpu.SemaphoreType.DMA((STAGES,)),
-            pltpu.SemaphoreType.DMA((STAGES,)),
-            pltpu.SemaphoreType.DMA((STAGES,)),
-            pltpu.SemaphoreType.DMA((STAGES,)),
+            pltpu.SemaphoreType.DMA((STAGES, PIECES, 2)),
+            pltpu.SemaphoreType.DMA((STAGES, PIECES, 2)),
+            pltpu.SemaphoreType.DMA((STAGES, 2, PER)),
+            pltpu.SemaphoreType.DMA((STAGES, 2, PER)),
+            pltpu.SemaphoreType.DMA((STAGES, PIECES)),
+            pltpu.SemaphoreType.DMA((STAGES, PIECES)),
+            pltpu.SemaphoreType.DMA((STAGES, PER)),
+            pltpu.SemaphoreType.DMA((STAGES, PER)),
+            pltpu.SemaphoreType.DMA((STAGES, PER)),
+            pltpu.SemaphoreType.DMA((STAGES, PER)),
+            pltpu.VMEM((part, slab, size_y), F32),
         ],
         compiler_params=pltpu.CompilerParams(
             collective_id=0, has_side_effects=True, vmem_limit_bytes=56 * 2**20
@@ -364,7 +383,7 @@
         observed,
         kernel_x.reshape(1, -1), kernel_y.reshape(1, -1), kernel_z.reshape(1, -1),
     )
-    return jnp.swapaxes(out, 0, 1)
+    return out
 
 
 def solution(mesh):

time: 163 us -> 136 us (0.83); the launches traced: 161 us -> 136 us
  Pallas kernels: 157 us -> 133 us
    pallas_call x1, Pallas kernels: 157 us -> 133 us  [shards(): pl.pallas_call(functools.partial(kernel, nz, nx), out_shape=jax.ShapeDtyp...]
    transpose x1 -> x0, local copies, waits for them, and re-layouts: 4.13 us -> none  [shards(): return jnp.swapaxes(out, 0, 1)]
    unnamed x0 -> x1, local copies, waits for them, and re-layouts: none -> 3.13 us
where the time goes in v3:
time: 136 us
  Pallas kernels  133 us (98%)
  local copies, waits for them, and re-layouts  3.13 us (2%)
    pallas_call x1, Pallas kernels, shards(): pl.pallas_call(functools.partial(kernel, nz, nx), out_shape=jax.ShapeDtyp...  133 us
    unnamed x1, local copies, waits for them, and re-layouts  3.13 us

profile of v3, /device:TPU:98, one launch (start us, length us, event | category | flops | bytes accessed | tf_op | source)
XLA Modules:
  0.0 135.8 jit_solution(14674664394886733602)
XLA Ops:
  0.0 132.6 %deconvolve.1 = f32[32,64,256]{2,1,0:T(8,128)} custom-call(f32[32,64,256]{2,1,0:T(8,128)} %obs_ref.1, f32[1,33]{1,0:T(1,128)} %bitcast.3, f32[1,33]{1,0:T(1,128)} %bitcast.4, f32[1,65]{1,0:T(1,128)} %bitcast.5), custom_call_target="tpu_custom_call" | custom-call | tf_op jit(solution)/shard_map/deconvolve/pallas_call | solution.py:352
  132.7 3.1 %copy.6 = f32[32,64,256]{2,1,0:T(8,128)} copy(f32[32,64,256]{2,1,0:T(8,128)} %deconvolve.1) | data formatting | bytes 4194304

commit v4 on v3

--- a/solution.py
+++ b/solution.py
@@ -12,7 +12,8 @@
 PIECES = 8
 PER = PIECES // CHUNKS
 RING = 4
-Z_DIRECT, X_DIRECT = 4, 5
+Z_DIRECT, X_DIRECT = 5, 4
+X_ROUTES = ((4, 2), (6, 2))
 MESH = pl.DeviceIdType.MESH
 BF, F32 = jnp.bfloat16, jnp.float32
 
@@ -58,17 +59,22 @@
     has_near = jnp.logical_and(gx > 0, gx < nx - 1)
 
     mid = nz // 2
-    seam_l, seam_r = zg == mid, zg == mid - 1
-    z_end = jnp.logical_or(zg == 0, zg == nz - 1)
-    z_seam = jnp.logical_or(seam_l, seam_r)
     place_x = lax.rem(gx, RING)
-    low_x, high_x = place_x == 0, place_x == RING - 1
-    x_end = jnp.logical_or(low_x, high_x)
+    x_end = jnp.logical_or(place_x == 0, place_x == RING - 1)
+
+    def corner(at):
+        return zg == at
+
+    seam_l, seam_r, first_z, last_z = corner(mid), corner(mid - 1), corner(0), corner(nz - 1)
+    z_end, z_seam = jnp.logical_or(first_z, last_z), jnp.logical_or(seam_l, seam_r)
     turn = (1 - 2 * odd) * (RING - 1)
     over = RING * (1 - 2 * odd)
+    skip = 2 * (1 - 2 * odd)
     x_seam = jnp.logical_and(x_end, has_near)
     x_forward = jnp.logical_and(x_end, jnp.logical_and(gx + over >= 0, gx + over < nx))
     x_from = jnp.logical_and(x_end, jnp.logical_and(gx - over >= 0, gx - over < nx))
+    x_inner = jnp.logical_and(jnp.logical_not(x_end), jnp.logical_and(gx + skip >= 0, gx + skip < nx))
+    x_ways = (x_forward, x_inner)
 
     barrier = pltpu.get_barrier_semaphore()
     peers = (
@@ -76,6 +82,7 @@
         ((jnp.where(z_end, mid, 0), gx), jnp.logical_or(z_end, z_seam)),
         ((jnp.where(z_end, mid - 1, nz - 1), gx), jnp.logical_or(z_end, z_seam)),
         ((zg, gx + turn), x_end), ((zg, gx + over), x_forward), ((zg, gx - over), x_from),
+        ((zg, gx + skip), x_inner), ((zg, gx - skip), x_from),
     )
     for peer, there in peers:
         @pl.when(there)
@@ -108,7 +115,7 @@
             device_id=(to, gx), device_id_type=MESH,
         )
 
-    z_sides = ((0, has_l, seam_l, zg == nz - 1), (1, has_r, seam_r, zg == 0))
+    z_sides = ((0, has_l, seam_l, last_z), (1, has_r, seam_r, first_z))
 
     def z_start(s, c):
         for side, there, seam, _ in z_sides:
@@ -153,17 +160,18 @@
                 z_copy(s, c, side, Z_DIRECT).wait_recv()
                 z_hop(s, c, side, 1).wait_recv()
 
-    def x_hop(s, p, hop):
-        n = piece - X_DIRECT
+    def x_hop(s, p, way, hop):
+        lo, n = X_ROUTES[way]
+        keep = xfw.at[s, p, pl.ds(lo - X_DIRECT, n)]
         if hop == 0:
-            src, dst, to = g.at[s, pl.ds(hx + head(p) + X_DIRECT, n)], xfw.at[s, p], gx + turn
+            src, dst, to = g.at[s, pl.ds(hx + head(p) + lo, n)], keep, (far if way else gx + turn)
             sems = xbsend, xfrecv
         else:
             at = (1 - odd) * (hx - piece * (p + 1)) + odd * (hx + cols + piece * p)
-            src, dst, to = xfw.at[s, p], g.at[s, pl.ds(at + X_DIRECT, n)], gx + over
+            src, dst, to = keep, g.at[s, pl.ds(at + lo, n)], gx + (skip if way else over)
             sems = xfsend, xbrecv
         return pltpu.make_async_remote_copy(
-            src_ref=src, dst_ref=dst, send_sem=sems[0].at[s, p], recv_sem=sems[1].at[s, p],
+            src_ref=src, dst_ref=dst, send_sem=sems[0].at[s, p, way], recv_sem=sems[1].at[s, p, way],
             device_id=(zg, to), device_id_type=MESH,
         )
 
@@ -182,10 +190,11 @@
         return jnp.logical_and(has_near, jnp.logical_not(x_seam))
 
     def x_forward_on(s, p):
-        @pl.when(x_forward)
-        def _():
-            x_hop(s, p, 0).wait_recv()
-            x_hop(s, p, 1).start()
+        for way, there in enumerate(x_ways):
+            @pl.when(there)
+            def _():
+                x_hop(s, p, way, 0).wait_recv()
+                x_hop(s, p, way, 1).start()
 
     def z_pass(s, c):
         z_arrived(s, c)
@@ -207,7 +216,8 @@
 
             @pl.when(x_seam)
             def _():
-                x_hop(s, c, 0).start()
+                for way in range(2):
+                    x_hop(s, c, way, 0).start()
                 x_copy(s, 0, c, X_DIRECT).start()
         if c >= PIECES - PER:
             x_copy(s, 1, c - (PIECES - PER)).start()
@@ -222,7 +232,8 @@
                 @pl.when(x_seam)
                 def _():
                     x_copy(s, 0, p, X_DIRECT).wait_recv()
-                    x_hop(s, p, 1).wait_recv()
+                    for way in range(2):
+                        x_hop(s, p, way, 1).wait_recv()
         if c == CHUNKS - 1:
             for p in range(PER):
                 x_copy(s, 1, p).wait_recv()
@@ -256,10 +267,21 @@
         def _():
             out_ref[:, pl.ds(pl.multiple_of(first(c), part), part)] = jnp.swapaxes(comb[2, rows, own] * v, 0, 1)
 
-        @pl.when(s < STAGES - 1)
+        late = CHUNKS - 2
+        go = s < STAGES - 1
+        if c == late:
+            go = s < STAGES - 2
+
+        @pl.when(go)
         def _():
             for p in range(PER):
                 z_start(s + 1, c * PER + p)
+
+        if c == CHUNKS - 1:
+            @pl.when(s == STAGES - 2)
+            def _():
+                for p in range(PER):
+                    z_start(s + 1, late * PER + p)
 
     for c in range(PIECES):
         xs = pl.ds(pl.multiple_of(head(c), piece), piece)
@@ -281,7 +303,7 @@
         wyh[d] = hi
         wyl[d] = lo
 
-    def stage(s, _):
+    def begin(s):
         zeros_z = jnp.zeros((1, hz, size_y), F32)
         zeros_x = jnp.zeros((1, slab, size_y), F32)
 
@@ -304,9 +326,12 @@
         z_pass(s, 2)
         x_forward_on(s, 1)
 
+    def stage(s, _):
+        begin(s)
+
         @pl.when(s > 0)
         def _():
-            xy_pass(s - 1, CHUNKS - 1)
+            xy_pass(s - 1, 3)
 
         z_pass(s, 3)
         z_pass(s, 4)
@@ -318,8 +343,19 @@
         xy_pass(s, 2)
         return 0
 
-    lax.fori_loop(0, STAGES, stage, 0)
-    xy_pass(STAGES - 1, CHUNKS - 1)
+    lax.fori_loop(0, STAGES - 1, stage, 0)
+    s = STAGES - 1
+    begin(s)
+    xy_pass(s - 1, 3)
+    z_pass(s, 3)
+    z_pass(s, 6)
+    z_pass(s, 7)
+    xy_pass(s, 0)
+    z_pass(s, 4)
+    z_pass(s, 5)
+    xy_pass(s, 1)
+    xy_pass(s, 2)
+    xy_pass(s, 3)
 
     def drain(s, _):
         for c in range(PIECES):
@@ -333,11 +369,13 @@
             @pl.when(x_seam)
             def _():
                 x_copy(s, 0, p, X_DIRECT).wait_send()
-                x_hop(s, p, 0).wait_send()
-
-            @pl.when(x_forward)
-            def _():
-                x_hop(s, p, 1).wait_send()
+                for way in range(2):
+                    x_hop(s, p, way, 0).wait_send()
+
+            for way, there in enumerate(x_ways):
+                @pl.when(there)
+                def _():
+                    x_hop(s, p, way, 1).wait_send()
 
             x_copy(s, 1, p).wait_send()
         return 0
@@ -351,7 +389,7 @@
     wide = slab * 3
     out = pl.pallas_call(
         functools.partial(kernel, nz, nx),
-        out_shape=jax.ShapeDtypeStruct((slab, cols, size_y), F32),
+        out_shape=pltpu.VMEM((slab, cols, size_y), F32),
         in_specs=[pl.BlockSpec(memory_space=pltpu.VMEM)] * 4,
         out_specs=pl.BlockSpec(memory_space=pltpu.VMEM),
         scratch_shapes=[
@@ -369,10 +407,10 @@
             pltpu.SemaphoreType.DMA((STAGES, 2, PER)),
             pltpu.SemaphoreType.DMA((STAGES, PIECES)),
             pltpu.SemaphoreType.DMA((STAGES, PIECES)),
-            pltpu.SemaphoreType.DMA((STAGES, PER)),
-            pltpu.SemaphoreType.DMA((STAGES, PER)),
-            pltpu.SemaphoreType.DMA((STAGES, PER)),
-            pltpu.SemaphoreType.DMA((STAGES, PER)),
+            pltpu.SemaphoreType.DMA((STAGES, PER, 2)),
+            pltpu.SemaphoreType.DMA((STAGES, PER, 2)),
+            pltpu.SemaphoreType.DMA((STAGES, PER, 2)),
+            pltpu.SemaphoreType.DMA((STAGES, PER, 2)),
             pltpu.VMEM((part, slab, size_y), F32),
         ],
         compiler_params=pltpu.CompilerParams(
@@ -383,7 +421,27 @@
         observed,
         kernel_x.reshape(1, -1), kernel_y.reshape(1, -1), kernel_z.reshape(1, -1),
     )
-    return out
+    return pl.pallas_call(
+        hand_over,
+        out_shape=jax.ShapeDtypeStruct(out.shape, F32),
+        in_specs=[pl.BlockSpec(memory_space=pltpu.VMEM)],
+        out_specs=pl.BlockSpec(memory_space=pl.ANY),
+        scratch_shapes=[pltpu.SemaphoreType.DMA((4,))],
+        compiler_params=pltpu.CompilerParams(vmem_limit_bytes=8 * 2**20),
+        name="hand_over",
+    )(out)
+
+
+def hand_over(src_ref, dst_ref, sem):
+    n = src_ref.shape[0] // 4
+    copies = [
+        pltpu.make_async_copy(src_ref.at[pl.ds(k * n, n)], dst_ref.at[pl.ds(k * n, n)], sem.at[k])
+        for k in range(4)
+    ]
+    for copy in copies:
+        copy.start()
+    for copy in copies:
+        copy.wait()
 
 
 def solution(mesh):

time: 136 us -> 128 us (0.941)
  Pallas kernels: 133 us -> 127 us
  local copies, waits for them, and re-layouts: 3.13 us -> 0 us
    pallas_call x1 -> x2, Pallas kernels: 133 us -> 127 us  [the longest x1 126 us: shards(): pl.pallas_call(functools.partial(kernel, nz, nx), out_shape=pltpu.VMEM((s...]
    unnamed x1 -> x0, local copies, waits for them, and re-layouts: 3.13 us -> none
where the time goes in v4:
time: 128 us
  Pallas kernels  127 us (99%)
    pallas_call x1, Pallas kernels, shards(): pl.pallas_call(functools.partial(kernel, nz, nx), out_shape=pltpu.VMEM((s...  126 us

profile of v4, /device:TPU:98, one launch (start us, length us, event | category | flops | bytes accessed | tf_op | source)
XLA Modules:
  0.0 127.6 jit_solution(14423731547762701502)
XLA Ops:
  0.0 126.1 %deconvolve.1.src_ref = f32[32,64,256]{2,1,0:T(8,128)S(1)} custom-call(f32[32,64,256]{2,1,0:T(8,128)} %obs_ref.1, f32[1,33]{1,0:T(1,128)} %bitcast.3, f32[1,33]{1,0:T(1,128)} %bitcast.4, f32[1,65]{1,0:T(1,128)} %bitcast.5), custom_call_target="tpu_custom_call" | custom-call | tf_op jit(solution)/shard_map/deconvolve/pallas_call | solution.py:390
  126.1 1.3 %hand_over.1 = f32[32,64,256]{2,1,0:T(8,128)} custom-call(f32[32,64,256]{2,1,0:T(8,128)S(1)} %deconvolve.1.src_ref), custom_call_target="tpu_custom_call" | custom-call | tf_op jit(solution)/shard_map/hand_over/pallas_call | solution.py:424

commit v5 on v4

--- a/solution.py
+++ b/solution.py
@@ -12,8 +12,8 @@
 PIECES = 8
 PER = PIECES // CHUNKS
 RING = 4
-Z_DIRECT, X_DIRECT = 5, 4
-X_ROUTES = ((4, 2), (6, 2))
+Z_DIRECT, X_DIRECT = 5, 3
+X_ROUTES = ((3, 3), (6, 2))
 MESH = pl.DeviceIdType.MESH
 BF, F32 = jnp.bfloat16, jnp.float32
 
@@ -45,7 +45,7 @@
     return pltpu.roll(wide, 0, 1, stride=1, stride_axis=0)
 
 
-def kernel(nz, nx, obs_ref, kx_ref, ky_ref, kz_ref, out_ref, comb, g, zfw, xfw, wz, wx, wyh, wyl,
+def kernel(nz, nx, obs_ref, kx_ref, ky_ref, kz_ref, out_ref, comb, g, zfw, xfw, wz, wx, wx8, wyh, wyl,
            zsend, zrecv, xsend, xrecv, zbsend, zbrecv, xbsend, xbrecv, xfsend, xfrecv, xdone):
     slab, cols, size_y = out_ref.shape
     part, piece = cols // CHUNKS, cols // PIECES
@@ -222,66 +222,77 @@
         if c >= PIECES - PER:
             x_copy(s, 1, c - (PIECES - PER)).start()
 
+    def near_arrived(s, p):
+        @pl.when(near_plain())
+        def _():
+            x_copy(s, 0, p).wait_recv()
+
+        @pl.when(x_seam)
+        def _():
+            x_copy(s, 0, p, X_DIRECT).wait_recv()
+            for way in range(2):
+                x_hop(s, p, way, 1).wait_recv()
+
+    def lateral(s, at, width, band):
+        d = lax.rem(s, 2)
+        rows = pl.ds(at, width)
+        n = width * 8
+
+        def group(k, _):
+            zs = pl.ds(pl.multiple_of(k * 8, 8), 8)
+            hi, lo = split(g[s, pl.ds(at, width + 2 * hx), zs].reshape((width + 2 * hx) * 8, size_y))
+            top = mxu(band[d], hi)
+            v = top[:n] + top[n:] + mxu(band[d, :n], lo)
+            xdone[:width, zs] = v.reshape(width, 8, size_y)
+            return 0
+
+        lax.fori_loop(0, slab // 8, group, 0, unroll=4)
+        hi, lo = split(xdone[:width].reshape(width * slab, size_y))
+        v = mxu(hi, wyh[d]) + mxu(lo, wyh[d]) + mxu(hi, wyl[d])
+        v = v.reshape(width, slab, size_y)
+        own = pl.ds(hz, slab)
+
+        @pl.when(d == 0)
+        def _():
+            comb[s + 1, rows, own] = comb[0, rows, own] / v
+
+        @pl.when(s == 1)
+        def _():
+            comb[2, rows, own] = comb[0, rows, own] * v
+
+        @pl.when(s == STAGES - 1)
+        def _():
+            out_ref[:, pl.ds(pl.multiple_of(at, width), width)] = jnp.swapaxes(comb[2, rows, own] * v, 0, 1)
+
+    def send_on(s, c):
+        late = CHUNKS - 2
+
+        @pl.when(s < STAGES - (2 if c == late else 1))
+        def _():
+            for p in range(PER):
+                z_start(s + 1, c * PER + p)
+
+        if c == CHUNKS - 1:
+            @pl.when(s == STAGES - 2)
+            def _():
+                for p in range(PER):
+                    z_start(s + 1, late * PER + p)
+
     def xy_pass(s, c):
-        if c == 0:
-            for p in range(PER):
-                @pl.when(near_plain())
-                def _():
-                    x_copy(s, 0, p).wait_recv()
-
-                @pl.when(x_seam)
-                def _():
-                    x_copy(s, 0, p, X_DIRECT).wait_recv()
-                    for way in range(2):
-                        x_hop(s, p, way, 1).wait_recv()
         if c == CHUNKS - 1:
             for p in range(PER):
                 x_copy(s, 1, p).wait_recv()
-        d = lax.rem(s, 2)
-        rows = pl.ds(first(c), part)
-        n = part * 8
-
-        def group(k, _):
-            zs = pl.ds(pl.multiple_of(k * 8, 8), 8)
-            hi, lo = split(g[s, pl.ds(first(c), part + 2 * hx), zs].reshape((part + 2 * hx) * 8, size_y))
-            top = mxu(wx[d], hi)
-            v = top[:n] + top[n:] + mxu(wx[d, :n], lo)
-            xdone[:, zs] = v.reshape(part, 8, size_y)
-            return 0
-
-        lax.fori_loop(0, slab // 8, group, 0, unroll=4)
-        hi, lo = split(xdone[...].reshape(part * slab, size_y))
-        v = mxu(hi, wyh[d]) + mxu(lo, wyh[d]) + mxu(hi, wyl[d])
-        v = v.reshape(part, slab, size_y)
-        own = pl.ds(hz, slab)
-
-        @pl.when(d == 0)
-        def _():
-            comb[s + 1, rows, own] = comb[0, rows, own] / v
-
-        @pl.when(s == 1)
-        def _():
-            comb[2, rows, own] = comb[0, rows, own] * v
-
-        @pl.when(s == STAGES - 1)
-        def _():
-            out_ref[:, pl.ds(pl.multiple_of(first(c), part), part)] = jnp.swapaxes(comb[2, rows, own] * v, 0, 1)
-
-        late = CHUNKS - 2
-        go = s < STAGES - 1
-        if c == late:
-            go = s < STAGES - 2
-
-        @pl.when(go)
-        def _():
-            for p in range(PER):
-                z_start(s + 1, c * PER + p)
-
-        if c == CHUNKS - 1:
-            @pl.when(s == STAGES - 2)
-            def _():
-                for p in range(PER):
-                    z_start(s + 1, late * PER + p)
+        lateral(s, first(c), part, wx)
+        send_on(s, c)
+
+    def near_inner(s):
+        near_arrived(s, 0)
+        lateral(s, head(1), piece, wx8)
+
+    def near_edge(s):
+        near_arrived(s, 1)
+        lateral(s, head(0), piece, wx8)
+        send_on(s, 0)
 
     for c in range(PIECES):
         xs = pl.ds(pl.multiple_of(head(c), piece), piece)
@@ -298,6 +309,9 @@
         hi, lo = split(toeplitz(place(kx_ref[...], 8 * (part + 2 * hx), 8, 0, rev), part * 8))
         wx[d, :part * 8] = hi
         wx[d, part * 8:] = lo
+        n, k = piece * 8, 8 * (piece + 2 * hx)
+        wx8[d, :n] = hi[:n, :k]
+        wx8[d, n:] = lo[:n, :k]
         half = ky_ref.shape[1] // 2
         hi, lo = split(toeplitz(place(ky_ref[...], size_y + 256, 1, 128 - half, not rev), size_y)[:, 128:128 + size_y])
         wyh[d] = hi
@@ -334,8 +348,9 @@
             xy_pass(s - 1, 3)
 
         z_pass(s, 3)
+        near_inner(s)
         z_pass(s, 4)
-        xy_pass(s, 0)
+        near_edge(s)
         z_pass(s, 5)
         xy_pass(s, 1)
         z_pass(s, 6)
@@ -350,7 +365,8 @@
     z_pass(s, 3)
     z_pass(s, 6)
     z_pass(s, 7)
-    xy_pass(s, 0)
+    near_inner(s)
+    near_edge(s)
     z_pass(s, 4)
     z_pass(s, 5)
     xy_pass(s, 1)
@@ -399,6 +415,7 @@
             pltpu.VMEM((STAGES, PER, piece - X_DIRECT, slab, size_y), F32),
             pltpu.VMEM((2, 2 * slab, wide), BF),
             pltpu.VMEM((2, 16 * part, 24 * part), BF),
+            pltpu.VMEM((2, 16 * piece, 8 * (piece + 2 * part)), BF),
             pltpu.VMEM((2, size_y, size_y), BF),
             pltpu.VMEM((2, size_y, size_y), BF),
             pltpu.SemaphoreType.DMA((STAGES, PIECES, 2)),

time: 128 us -> 126 us (0.984); the launches traced: 128 us -> 124 us
  Pallas kernels: 127 us -> 124 us
    pallas_call x1, Pallas kernels: 126 us -> 122 us  [shards(): pl.pallas_call(functools.partial(kernel, nz, nx), out_shape=pltpu.VMEM((s...]
where the time goes in v5:
time: 126 us; the launch traced here: 124 us
  Pallas kernels  124 us (98%)
    pallas_call x1, Pallas kernels, shards(): pl.pallas_call(functools.partial(kernel, nz, nx), out_shape=pltpu.VMEM((s...  122 us

profile of v5, /device:TPU:98, one launch (start us, length us, event | category | flops | bytes accessed | tf_op | source)
XLA Modules:
  0.0 123.8 jit_solution(8916078758353491692)
XLA Ops:
  0.0 122.3 %deconvolve.1.src_ref = f32[32,64,256]{2,1,0:T(8,128)S(1)} custom-call(f32[32,64,256]{2,1,0:T(8,128)} %obs_ref.1, f32[1,33]{1,0:T(1,128)} %bitcast.3, f32[1,33]{1,0:T(1,128)} %bitcast.4, f32[1,65]{1,0:T(1,128)} %bitcast.5), custom_call_target="tpu_custom_call" | custom-call | tf_op jit(solution)/shard_map/deconvolve/pallas_call | solution.py:406
  122.3 1.3 %hand_over.1 = f32[32,64,256]{2,1,0:T(8,128)} custom-call(f32[32,64,256]{2,1,0:T(8,128)S(1)} %deconvolve.1.src_ref), custom_call_target="tpu_custom_call" | custom-call | tf_op jit(solution)/shard_map/hand_over/pallas_call | solution.py:441

commit v6 on v5

--- a/solution.py
+++ b/solution.py
@@ -46,7 +46,7 @@
 
 
 def kernel(nz, nx, obs_ref, kx_ref, ky_ref, kz_ref, out_ref, comb, g, zfw, xfw, wz, wx, wx8, wyh, wyl,
-           zsend, zrecv, xsend, xrecv, zbsend, zbrecv, xbsend, xbrecv, xfsend, xfrecv, xdone):
+           zsend, zrecv, xsend, xrecv, zbsend, zbrecv, xbsend, xbrecv, xfsend, xfrecv, xdone, loaded, loadsem):
     slab, cols, size_y = out_ref.shape
     part, piece = cols // CHUNKS, cols // PIECES
     hz, hx = slab, part
@@ -76,6 +76,16 @@
     x_inner = jnp.logical_and(jnp.logical_not(x_end), jnp.logical_and(gx + skip >= 0, gx + skip < nx))
     x_ways = (x_forward, x_inner)
 
+    def head(p):
+        return piece * (p + odd * (PIECES - 1 - 2 * p))
+
+    def load(c):
+        xs = pl.ds(pl.multiple_of(head(c), piece), piece)
+        return pltpu.make_async_copy(obs_ref.at[:, xs], loaded.at[:, xs], loadsem.at[c])
+
+    for c in range(PIECES):
+        load(c).start()
+
     barrier = pltpu.get_barrier_semaphore()
     peers = (
         ((zg - 1, gx), has_l), ((zg + 1, gx), has_r), ((zg, near), has_near), ((zg, far), gx >= 0),
@@ -91,9 +101,6 @@
 
     def first(c):
         return part * (c + odd * (CHUNKS - 1 - 2 * c))
-
-    def head(p):
-        return piece * (p + odd * (PIECES - 1 - 2 * p))
 
     def z_copy(s, c, side, n=piece):
         rows = pl.ds(head(c), n)
@@ -296,7 +303,8 @@
 
     for c in range(PIECES):
         xs = pl.ds(pl.multiple_of(head(c), piece), piece)
-        comb[0, xs, hz:hz + slab] = jnp.swapaxes(obs_ref[:, xs], 0, 1)
+        load(c).wait()
+        comb[0, xs, hz:hz + slab] = jnp.swapaxes(loaded[:, xs], 0, 1)
         if c == 0:
             pl.semaphore_wait(barrier, sum(there.astype(jnp.int32) for _, there in peers))
         z_start(0, c)
@@ -317,7 +325,7 @@
         wyh[d] = hi
         wyl[d] = lo
 
-    def begin(s):
+    def clear(s):
         zeros_z = jnp.zeros((1, hz, size_y), F32)
         zeros_x = jnp.zeros((1, slab, size_y), F32)
 
@@ -334,6 +342,7 @@
         fill(gx == 0, g, 0, hx, pl.ds(0, slab), zeros_x)
         fill(gx == nx - 1, g, hx + cols, hx, pl.ds(0, slab), zeros_x)
 
+    def begin(s):
         z_pass(s, 0)
         z_pass(s, 1)
         x_forward_on(s, 0)
@@ -348,16 +357,18 @@
             xy_pass(s - 1, 3)
 
         z_pass(s, 3)
+        z_pass(s, 4)
         near_inner(s)
-        z_pass(s, 4)
+        z_pass(s, 5)
         near_edge(s)
-        z_pass(s, 5)
         xy_pass(s, 1)
         z_pass(s, 6)
         z_pass(s, 7)
         xy_pass(s, 2)
+        clear(s + 1)
         return 0
 
+    clear(0)
     lax.fori_loop(0, STAGES - 1, stage, 0)
     s = STAGES - 1
     begin(s)
@@ -406,7 +417,7 @@
     out = pl.pallas_call(
         functools.partial(kernel, nz, nx),
         out_shape=pltpu.VMEM((slab, cols, size_y), F32),
-        in_specs=[pl.BlockSpec(memory_space=pltpu.VMEM)] * 4,
+        in_specs=[pl.BlockSpec(memory_space=pltpu.HBM)] + [pl.BlockSpec(memory_space=pltpu.VMEM)] * 3,
         out_specs=pl.BlockSpec(memory_space=pltpu.VMEM),
         scratch_shapes=[
             pltpu.VMEM((STAGES, cols, wide, size_y), F32),
@@ -429,6 +440,8 @@
             pltpu.SemaphoreType.DMA((STAGES, PER, 2)),
             pltpu.SemaphoreType.DMA((STAGES, PER, 2)),
             pltpu.VMEM((part, slab, size_y), F32),
+            pltpu.VMEM((slab, cols, size_y), F32),
+            pltpu.SemaphoreType.DMA((PIECES,)),
         ],
         compiler_params=pltpu.CompilerParams(
             collective_id=0, has_side_effects=True, vmem_limit_bytes=56 * 2**20

time: 126 us -> 125 us (level); the launches traced: 124 us -> 125 us
  no operation moved by 1% of the time
where the time goes in v6:
time: 125 us
  Pallas kernels  125 us (100%)
    pallas_call x1, Pallas kernels, shards(): pl.pallas_call(functools.partial(kernel, nz, nx), out_shape=pltpu.VMEM((s...  123 us

profile of v6, /device:TPU:98, one launch (start us, length us, event | category | flops | bytes accessed | tf_op | source)
XLA Modules:
  0.0 124.9 jit_solution(2761813203470735237)
XLA Ops:
  0.0 123.4 %deconvolve.1.src_ref = f32[32,64,256]{2,1,0:T(8,128)S(1)} custom-call(f32[32,64,256]{2,1,0:T(8,128)} %obs_ref.1, f32[1,33]{1,0:T(1,128)} %bitcast.3, f32[1,33]{1,0:T(1,128)} %bitcast.4, f32[1,65]{1,0:T(1,128)} %bitcast.5), custom_call_target="tpu_custom_call" | custom-call | tf_op jit(solution)/shard_map/deconvolve/pallas_call | solution.py:417
  123.4 1.3 %hand_over.1 = f32[32,64,256]{2,1,0:T(8,128)} custom-call(f32[32,64,256]{2,1,0:T(8,128)S(1)} %deconvolve.1.src_ref), custom_call_target="tpu_custom_call" | custom-call | tf_op jit(solution)/shard_map/hand_over/pallas_call | solution.py:454
